TPU v7x, 32 devices: a whole 2x2x4 slice. The times are simulated.
32 devices in a mesh: dp: 2 (over core), context: 4 (over y, x), tensor: 4 (over z).
Axes of the slice: x: 2, y: 2, z: 4, core: 2. Of those that a mesh axis runs over, the one named last changes fastest.
Arguments:
- inputs: bfloat16 [3072, 1024], P(('dp', 'context')), may hold values from -6 to 6
- cotangent: bfloat16 [3072, 1024], P(('dp', 'context')), may hold values from -6 to 6
- initial_state: float32 [2, 4, 128, 256], P('dp', 'tensor'), may hold values from -6 to 6
- norm_one: float32 [1024], replicated, may hold values from 0.5 to 1.5
- query_weight: bfloat16 [1024, 512], P(('dp', 'context'), 'tensor'), may hold values from -0.1875 to 0.1875
- key_weight: bfloat16 [1024, 512], P(('dp', 'context'), 'tensor'), may hold values from -0.1875 to 0.1875
- value_weight: bfloat16 [1024, 1024], P(('dp', 'context'), 'tensor'), may hold values from -0.1875 to 0.1875
- outgate_weight: bfloat16 [1024, 1024], P(('dp', 'context'), 'tensor'), may hold values from -0.1875 to 0.1875
- output_weight: bfloat16 [1024, 1024], P(('dp', 'context'), 'tensor'), may hold values from -0.375 to 0.375
- lowrank_weight: bfloat16 [1024, 16], replicated, may hold values from -0.1875 to 0.1875
- rankup_weight: bfloat16 [16, 512], P(None, 'tensor'), may hold values from -1.5 to 1.5
- gate_bias: float32 [512], P('tensor'), may hold values from 0.5 to 8
- head_gain: float32 [256], replicated, may hold values from 0.5 to 1.5
- norm_two: float32 [1024], replicated, may hold values from 0.5 to 1.5
- gate_weight: bfloat16 [1024, 2816], P(('dp', 'context'), 'tensor'), may hold values from -0.1875 to 0.1875
- up_weight: bfloat16 [1024, 2816], P(('dp', 'context'), 'tensor'), may hold values from -0.1875 to 0.1875
- down_weight: bfloat16 [1024, 2816], P(('dp', 'context'), 'tensor'), may hold values from -0.21875 to 0.21875
Outputs:
- outputs: bfloat16 [3072, 1024], P(('dp', 'context'))
- grad_inputs: float32 [3072, 1024], P(('dp', 'context'))
- grad_norm_one: float32 [1024], replicated
- grad_query: float32 [1024, 512], P(('dp', 'context'), 'tensor')
- grad_key: float32 [1024, 512], P(('dp', 'context'), 'tensor')
- grad_value: float32 [1024, 1024], P(('dp', 'context'), 'tensor')
- grad_outgate: float32 [1024, 1024], P(('dp', 'context'), 'tensor')
- grad_output: float32 [1024, 1024], P(('dp', 'context'), 'tensor')
- grad_lowrank: float32 [1024, 16], replicated
- grad_rankup: float32 [16, 512], P(None, 'tensor')
- grad_bias: float32 [512], P('tensor')
- grad_head_gain: float32 [256], replicated
- grad_norm_two: float32 [1024], replicated
- grad_gate: float32 [1024, 2816], P(('dp', 'context'), 'tensor')
- grad_up: float32 [1024, 2816], P(('dp', 'context'), 'tensor')
- grad_down: float32 [1024, 2816], P(('dp', 'context'), 'tensor')
All inputs are finite; a program needn't handle non-finite values.
Results may differ from a plain program's by a relative error of at most 0.011.
The roundings to bfloat16 on the way count: a program that leaves them out, or rounds other values in their place, can miss the bound.
Values may be sent and summed in bfloat16 or wider, within the bound.
No kernel may reach another device: no remote copies, remote signals or barrier semaphores. Data moves between devices by JAX's collectives and lax.ppermute only.
A program may use at most 128 MiB of HBM per device.

v0:
```python
import jax
import jax.numpy as jnp
from jax import lax
from jax.sharding import PartitionSpec as P

DK = 512
RANK = 16
GROUP = 64
HEAD_K = 128
HEAD_V = 256
highest_precision = lax.Precision.HIGHEST
epsilon = 1e-06


def carried_in(value, axis, join, neutral, backward):
    count, mine = (lax.axis_size(axis), lax.axis_index(axis))
    pieces = jax.tree.map(lambda part: lax.all_gather(part, axis), value)
    if backward:
        pieces = jax.tree.map(lambda part: part[::-1], pieces)
        mine = count - 1 - mine
    so_far = jax.tree.map(
        lambda part, zero: jnp.full_like(part, 0) + jnp.asarray(zero, part.dtype), value, neutral
    )

    def step(position, so_far):
        longer = join(so_far, jax.tree.map(lambda part: part[position], pieces))
        return jax.tree.map(lambda new, old: jnp.where(position < mine, new, old), longer, so_far)

    return lax.fori_loop(0, count - 1, step, so_far)


def rms_scale(vectors, gain):
    inverse = lax.rsqrt(jnp.mean(vectors * vectors, axis=-1, keepdims=True) + epsilon)
    return vectors * inverse * gain


def rms_back(vectors, gain, upstream):
    inverse = lax.rsqrt(jnp.mean(vectors * vectors, axis=-1, keepdims=True) + epsilon)
    normal_part = vectors * inverse
    scaled_up = upstream * gain
    back_vectors = inverse * (
        scaled_up - normal_part * jnp.mean(scaled_up * normal_part, axis=-1, keepdims=True)
    )
    return (back_vectors, upstream * normal_part)


def project(left, weight):
    return jnp.dot(left, weight, preferred_element_type=jnp.float32)


def project_back(left, weight):
    return lax.dot_general(
        left, weight, (((1,), (1,)), ((), ())), preferred_element_type=jnp.float32
    )


def weight_grad(left, right):
    return lax.dot_general(
        left, right, (((0,), (0,)), ((), ())), preferred_element_type=jnp.float32
    )


def swish_slope(preact):
    sigma = jax.nn.sigmoid(preact)
    return sigma * (1.0 + preact * (1.0 - sigma))


def gla_core(query, keys, values, log_decay):
    length = keys.shape[0]
    blocks = length // GROUP
    causal = jnp.tril(jnp.ones((GROUP, GROUP), jnp.float32))

    def advance(state, pieces):
        query_blk, key_blk, value_blk, decay_blk = pieces
        running = jnp.cumsum(decay_blk, axis=0)
        ending = running[-1]
        query_up = query_blk * jnp.exp(running)
        key_down = key_blk * jnp.exp(-running)
        scores = jnp.dot(query_up, key_down.T, precision=highest_precision) * causal
        within = jnp.dot(scores, value_blk, precision=highest_precision) + jnp.dot(
            query_up, state, precision=highest_precision
        )
        key_tail = key_blk * jnp.exp(ending - running)
        state = jnp.exp(ending)[:, None] * state + jnp.dot(
            key_tail.T, value_blk, precision=highest_precision
        )
        return (state, within)

    start_state = jnp.zeros((keys.shape[1], values.shape[1]), jnp.float32)
    final_state, pieces_out = lax.scan(
        advance,
        start_state,
        (
            query.reshape(blocks, GROUP, -1),
            keys.reshape(blocks, GROUP, -1),
            values.reshape(blocks, GROUP, -1),
            log_decay.reshape(blocks, GROUP, -1),
        ),
    )
    return (pieces_out.reshape(length, values.shape[1]), final_state)


def core_heads(query, keys, values, log_decay):
    return jax.vmap(gla_core, in_axes=(1, 1, 1, 1), out_axes=(1, 0))(query, keys, values, log_decay)


def gate_norm(attention_result, outgate, head_gain):
    return rms_scale(attention_result, head_gain) * outgate * jax.nn.sigmoid(outgate)


def span_result(query, keys, values, log_decay, incoming_state):
    local_output, local_state = core_heads(query, keys, values, log_decay)
    running = jnp.cumsum(log_decay, axis=0)
    decayed_state = query * jnp.exp(running)
    carried_state = jnp.einsum(
        "xbd,bdy->xby", decayed_state, incoming_state, precision=highest_precision
    )
    outgoing = jnp.exp(running[-1])[:, :, None] * incoming_state + local_state
    return (local_output + carried_state, outgoing)


def chain_combine(earlier, later):
    return (earlier[0] * later[0], later[0][:, :, None] * earlier[1] + later[1])


def local(
    inputs,
    cotangent,
    initial_state,
    norm_one,
    query_weight,
    key_weight,
    value_weight,
    outgate_weight,
    output_weight,
    lowrank_weight,
    rankup_weight,
    gate_bias,
    head_gain,
    norm_two,
    gate_weight,
    up_weight,
    down_weight,
):
    fetched = (
        lax.all_gather(query_weight, ("dp", "context"), axis=0, tiled=True),
        lax.all_gather(key_weight, ("dp", "context"), axis=0, tiled=True),
        lax.all_gather(value_weight, ("dp", "context"), axis=0, tiled=True),
        lax.all_gather(outgate_weight, ("dp", "context"), axis=0, tiled=True),
        lax.all_gather(output_weight, ("dp", "context"), axis=0, tiled=True),
        lax.all_gather(gate_weight, ("dp", "context"), axis=0, tiled=True),
        lax.all_gather(up_weight, ("dp", "context"), axis=0, tiled=True),
        lax.all_gather(down_weight, ("dp", "context"), axis=0, tiled=True),
    )
    rows = inputs.shape[0]
    heads_here = fetched[0].shape[1] // HEAD_K
    scale = HEAD_K ** (-0.5)
    stream = inputs.astype(jnp.float32)
    normed_one = rms_scale(stream, norm_one).astype(jnp.bfloat16)
    query = (project(normed_one, fetched[0]) * scale).reshape(rows, heads_here, HEAD_K)
    keys = project(normed_one, fetched[1]).reshape(rows, heads_here, HEAD_K)
    values = project(normed_one, fetched[2]).reshape(rows, heads_here, HEAD_V)
    outgate = project(normed_one, fetched[3]).reshape(rows, heads_here, HEAD_V)
    lowrank = project(normed_one, lowrank_weight).astype(jnp.bfloat16)
    gate_logit = project(lowrank, rankup_weight) + gate_bias
    log_decay = (jax.nn.log_sigmoid(gate_logit) / 16.0).reshape(rows, heads_here, HEAD_K)
    local_output, local_state = core_heads(query, keys, values, log_decay)
    running = jnp.cumsum(log_decay, axis=0)
    decay_total = jnp.exp(running[-1])
    decayed_state = query * jnp.exp(running)
    prefix = carried_in(
        (decay_total, local_state),
        "context",
        chain_combine,
        (jnp.ones_like(decay_total), jnp.zeros_like(local_state)),
        False,
    )
    incoming_state = prefix[0][:, :, None] * initial_state[0] + prefix[1]
    attention_result = local_output + jnp.einsum(
        "xbd,bdy->xby", decayed_state, incoming_state, precision=highest_precision
    )
    gated = gate_norm(attention_result, outgate, head_gain).reshape(rows, -1).astype(jnp.bfloat16)
    hidden = stream + lax.psum(project_back(gated, fetched[4]), "tensor")
    normed_two = rms_scale(hidden, norm_two).astype(jnp.bfloat16)
    gate_input = project(normed_two, fetched[5])
    up_input = project(normed_two, fetched[6])
    product = (jax.nn.silu(gate_input) * up_input).astype(jnp.bfloat16)
    result = hidden + lax.psum(project_back(product, fetched[7]), "tensor")
    weights = (
        lax.all_gather(query_weight, ("dp", "context"), axis=0, tiled=True),
        lax.all_gather(key_weight, ("dp", "context"), axis=0, tiled=True),
        lax.all_gather(value_weight, ("dp", "context"), axis=0, tiled=True),
        lax.all_gather(outgate_weight, ("dp", "context"), axis=0, tiled=True),
        lax.all_gather(output_weight, ("dp", "context"), axis=0, tiled=True),
        lax.all_gather(gate_weight, ("dp", "context"), axis=0, tiled=True),
        lax.all_gather(up_weight, ("dp", "context"), axis=0, tiled=True),
        lax.all_gather(down_weight, ("dp", "context"), axis=0, tiled=True),
    )
    back_product = project(cotangent, weights[7])
    grad_down = weight_grad(cotangent, product)
    back_up = (back_product * jax.nn.silu(gate_input)).astype(jnp.bfloat16)
    back_gate = (back_product * up_input * swish_slope(gate_input)).astype(jnp.bfloat16)
    grad_gate = weight_grad(normed_two, back_gate)
    grad_up = weight_grad(normed_two, back_up)
    back_normed_two = lax.psum(
        project_back(back_gate, weights[5]) + project_back(back_up, weights[6]), "tensor"
    )
    back_hidden_norm, gain_two_rows = rms_back(hidden, norm_two, back_normed_two)
    back_hidden = cotangent.astype(jnp.float32) + back_hidden_norm
    back_low = back_hidden.astype(jnp.bfloat16)
    back_gated = project(back_low, weights[4])
    grad_output = weight_grad(back_low, gated)
    ignored, gate_pull = jax.vjp(gate_norm, attention_result, outgate, head_gain)
    attention_backward_pass, back_outgate, grad_head = gate_pull(
        back_gated.reshape(rows, heads_here, HEAD_V)
    )
    pending_state = jnp.einsum(
        "rjm,rjy->jmy", decayed_state, attention_backward_pass, precision=highest_precision
    )
    suffix = carried_in(
        (decay_total, pending_state),
        "context",
        chain_combine,
        (jnp.ones_like(decay_total), jnp.zeros_like(pending_state)),
        True,
    )
    ignored, span_pull = jax.vjp(span_result, query, keys, values, log_decay, incoming_state)
    back_query, back_keys, back_values, back_decay, back_incoming = span_pull(
        (attention_backward_pass, suffix[1])
    )
    low_query = (back_query.reshape(rows, -1) * scale).astype(jnp.bfloat16)
    low_keys = back_keys.reshape(rows, -1).astype(jnp.bfloat16)
    low_values = back_values.reshape(rows, -1).astype(jnp.bfloat16)
    low_outgate = back_outgate.reshape(rows, -1).astype(jnp.bfloat16)
    back_logit = back_decay.reshape(rows, -1) * jax.nn.sigmoid(-gate_logit) / 16.0
    grad_bias = jnp.sum(back_logit, axis=0)
    low_logit = back_logit.astype(jnp.bfloat16)
    grad_rankup = weight_grad(lowrank, low_logit)
    back_lowrank = jnp.einsum(
        "shk,rhk->shr",
        low_logit.reshape(rows, heads_here, HEAD_K),
        rankup_weight.reshape(RANK, heads_here, HEAD_K),
        preferred_element_type=jnp.float32,
    ).astype(jnp.bfloat16)
    grad_lowrank = jnp.einsum(
        "sd,shr->dr", normed_one, back_lowrank, preferred_element_type=jnp.float32
    )
    grad_query = weight_grad(normed_one, low_query)
    grad_key = weight_grad(normed_one, low_keys)
    grad_value = weight_grad(normed_one, low_values)
    grad_outgate = weight_grad(normed_one, low_outgate)
    partial_one = (
        project_back(low_query, weights[0])
        + project_back(low_keys, weights[1])
        + project_back(low_values, weights[2])
        + project_back(low_outgate, weights[3])
        + jnp.einsum("shr,dr->sd", back_lowrank, lowrank_weight, preferred_element_type=jnp.float32)
    )
    back_normed_one = lax.psum(partial_one, "tensor")
    back_stream, gain_one_rows = rms_back(stream, norm_one, back_normed_one)
    grad_inputs = back_hidden + back_stream
    quarter = rows // lax.axis_size("tensor")
    begin = lax.axis_index("tensor") * quarter
    gain_one_part = jnp.sum(lax.dynamic_slice_in_dim(gain_one_rows, begin, quarter, 0), axis=0)
    gain_two_part = jnp.sum(lax.dynamic_slice_in_dim(gain_two_rows, begin, quarter, 0), axis=0)
    columns = grad_rankup.shape[1]
    offset = lax.axis_index("tensor") * columns
    rank_full = lax.dynamic_update_slice(
        jnp.zeros((RANK, DK), jnp.float32), grad_rankup, (0, offset)
    )
    bias_full = lax.dynamic_update_slice(jnp.zeros((DK,), jnp.float32), grad_bias, (offset,))
    summed = lax.psum(
        (gain_one_part, gain_two_part, grad_head, grad_lowrank, rank_full, bias_full),
        ("dp", "context", "tensor"),
    )
    rankup_shard = lax.dynamic_slice(summed[4], (0, offset), (RANK, columns))
    bias_shard = lax.dynamic_slice(summed[5], (offset,), (columns,))
    shards = (
        lax.psum_scatter(grad_query, ("dp", "context"), scatter_dimension=0, tiled=True),
        lax.psum_scatter(grad_key, ("dp", "context"), scatter_dimension=0, tiled=True),
        lax.psum_scatter(grad_value, ("dp", "context"), scatter_dimension=0, tiled=True),
        lax.psum_scatter(grad_outgate, ("dp", "context"), scatter_dimension=0, tiled=True),
        lax.psum_scatter(grad_output, ("dp", "context"), scatter_dimension=0, tiled=True),
        lax.psum_scatter(grad_gate, ("dp", "context"), scatter_dimension=0, tiled=True),
        lax.psum_scatter(grad_up, ("dp", "context"), scatter_dimension=0, tiled=True),
        lax.psum_scatter(grad_down, ("dp", "context"), scatter_dimension=0, tiled=True),
    )
    return (
        result.astype(jnp.bfloat16),
        grad_inputs,
        summed[0],
        shards[0],
        shards[1],
        shards[2],
        shards[3],
        shards[4],
        summed[3],
        rankup_shard,
        bias_shard,
        summed[2],
        summed[1],
        shards[5],
        shards[6],
        shards[7],
    )


def solution(mesh):
    placed = (
        P(("dp", "context"), None),
        P(("dp", "context"), None),
        P("dp", "tensor", None, None),
        P(),
        P(("dp", "context"), "tensor"),
        P(("dp", "context"), "tensor"),
        P(("dp", "context"), "tensor"),
        P(("dp", "context"), "tensor"),
        P(("dp", "context"), "tensor"),
        P(),
        P(None, "tensor"),
        P("tensor"),
        P(),
        P(),
        P(("dp", "context"), "tensor"),
        P(("dp", "context"), "tensor"),
        P(("dp", "context"), "tensor"),
    )
    return jax.shard_map(
        local,
        mesh=mesh,
        in_specs=placed,
        out_specs=(
            P(("dp", "context"), None),
            P(("dp", "context"), None),
            P(),
            P(("dp", "context"), "tensor"),
            P(("dp", "context"), "tensor"),
            P(("dp", "context"), "tensor"),
            P(("dp", "context"), "tensor"),
            P(("dp", "context"), "tensor"),
            P(),
            P(None, "tensor"),
            P("tensor"),
            P(),
            P(),
            P(("dp", "context"), "tensor"),
            P(("dp", "context"), "tensor"),
            P(("dp", "context"), "tensor"),
        ),
        check_vma=False,
    )
```

profile of v0, /device:TPU:0, one launch (start us, length us, event | category | flops | bytes accessed | tf_op | source)
XLA Modules:
  0.0 835.5 jit_solution(9248610303740419045)
XLA Ops:
  9.5 2.5 convert_multiply_fusion
  13.6 25.4 %all_gather.52 = bf16[1024,128]{1,0:T(8,128)(2,1)S(1)} all-gather(bf16[128,128]{1,0:T(8,128)(2,1)S(1)} %copy-done.48), channel_id=1, replica_groups=mesh['dp'=2,'context'=4,'tensor'=4] {'dp','context'}, dimensions={0}, use_global_device_ids=true | all-gather | bytes 294912 | tf_op jit(solution)/shard_map/all_gather | solution.py:146
  39.7 24.6 %all_gather.51 = bf16[1024,256]{1,0:T(8,128)(2,1)S(1)} all-gather(bf16[128,256]{1,0:T(8,128)(2,1)S(1)} %copy-done.41), channel_id=1, replica_groups=mesh['dp'=2,'context'=4,'tensor'=4] {'dp','context'}, dimensions={0}, use_global_device_ids=true | all-gather | bytes 589824 | tf_op jit(solution)/shard_map/all_gather | solution.py:148
  64.7 23.7 %all_gather.50 = bf16[1024,128]{1,0:T(8,128)(2,1)S(1)} all-gather(bf16[128,128]{1,0:T(8,128)(2,1)S(1)} %copy-done.49), channel_id=1, replica_groups=mesh['dp'=2,'context'=4,'tensor'=4] {'dp','context'}, dimensions={0}, use_global_device_ids=true | all-gather | bytes 294912 | tf_op jit(solution)/shard_map/all_gather | solution.py:147
  89.1 7.0 while.106
  96.8 10.7 %all-gather = f32[4,128,256]{2,1,0:T(8,128)S(1)} all-gather(f32[1,128,256]{2,1,0:T(8,128)S(1)} %get-tuple-element.770), channel_id=2, replica_groups=mesh['dp'=2,'context'=4,'tensor'=4] {'context'}, dimensions={0}, use_global_device_ids=true | all-gather | bytes 655360 | tf_op jit(solution)/shard_map/all_gather | solution.py:17
  108.2 7.2 all_gather.53
  117.0 24.7 %all_gather.56 = bf16[1024,256]{1,0:T(8,128)(2,1)S(1)} all-gather(bf16[128,256]{1,0:T(8,128)(2,1)S(1)} %copy-done.42), channel_id=1, replica_groups=mesh['dp'=2,'context'=4,'tensor'=4] {'dp','context'}, dimensions={0}, use_global_device_ids=true | all-gather | bytes 589824 | tf_op jit(solution)/shard_map/all_gather | solution.py:149
  142.2 24.6 %all_gather.57 = bf16[1024,256]{1,0:T(8,128)(2,1)S(1)} all-gather(bf16[128,256]{1,0:T(8,128)(2,1)S(1)} %copy-done.43), channel_id=1, replica_groups=mesh['dp'=2,'context'=4,'tensor'=4] {'dp','context'}, dimensions={0}, use_global_device_ids=true | all-gather | bytes 589824 | tf_op jit(solution)/shard_map/all_gather | solution.py:150
  171.8 67.8 %all-reduce.9.cloned.1.call-done = f32[384,1024]{1,0:T(8,128)} async-done(((f32[384,1024]{1,0:T(8,128)}), f32[384,1024]{1,0:T(8,128)}) %all-reduce.9.cloned.1.call-update) | async-done | bytes 1572880 | tf_op jit(solution)/shard_map/psum | solution.py:183
  239.6 1.8 multiply_reduce_fusion.2
  242.6 4.2 fusion.171
  246.8 3.5 fusion.172
  251.6 4.4 multiply_convert_fusion.2
  257.8 2.0 convolution_add_fusion.3
  262.8 53.0 %while.109 = (s32[]{:T(128)}, f32[1,128,256]{2,1,0:T(8,128)S(1)}, f32[6,1,64,128]{3,2,1,0:T(8,128)}, f32[6,1,64,128]{3,2,1,0:T(8,128)}, f32[6,1,128,64]{2,3,1,0:...) while((s32[]{:T(128)}, f32[1,128,256]{2,1,0:T(8,128)S(1)}, ...), condition=%wide.region_19.20_spmd.clone.clone, body=%wide.region_17.19_spmd.clone.sunk.clone | while | flops 32215044 | bytes 1288872 | solution.py:90
  317.8 3.5 fusion.173
  321.3 7.6 all-reduce.11.cloned.1.call-done
  328.9 1.8 multiply_reduce_fusion.1
  331.0 1.9 multiply_add_fusion.1
  336.5 10.7 %all-gather.1 = f32[512,256]{1,0:T(8,128)} all-gather(f32[128,256]{1,0:T(8,128)S(1)} %fusion.128), channel_id=3, replica_groups=mesh['dp'=2,'context'=4,'tensor'=4] {'context'}, dimensions={0}, use_global_device_ids=true | all-gather | bytes 655360 | tf_op jit(solution)/shard_map/all_gather | solution.py:17
  347.2 1.9 rev.7
  349.1 3.1 while.108
  354.9 1.9 copy.112
  356.8 2.5 fusion.125
  361.4 115.1 %while.105 = (s32[]{:T(128)}, f32[1,128,256]{1,2,0:T(8,128)S(1)}, f32[6,1,64,128]{3,2,1,0:T(8,128)}, bf16[6,1,64,128]{3,2,1,0:T(8,128)(2,1)}, bf16[6,1,64,256]{3...) while((s32[]{:T(128)}, f32[1,128,256]{1,2,0:T(8,128)S(1)}, ...), condition=%wide.region_24.25_spmd.clone.clone, body=%wide.region_20.24_spmd.clone.sunk.clone | while | flops 139243520 | bytes 3109597 | solution.py:90
  364.0 1.7 copy.136
  378.8 1.7 fusion.345
  398.0 1.7 fusion.345
  417.2 1.7 fusion.345
  436.4 1.7 fusion.345
  455.6 1.7 fusion.345
  474.8 1.7 fusion.345
  476.5 1.9 fusion.144
  487.7 2.1 fusion.178
  489.8 2.1 fusion.179
  492.0 2.4 fusion.180
  494.5 2.4 fusion.132
  499.9 3.5 fusion.182
  503.5 3.6 fusion.183
  508.2 3.6 convolution_bitcast_fusion.5
  513.5 92.7 %all-reduce.15.cloned.1.call-done = (f32[384,1024]{1,0:T(8,128)}, f32[384,1024]{1,0:T(8,128)}) async-done(((f32[384,1024]{1,0:T(8,128)}, f32[384,1024]{1,0:T(8,128)}), (f32[384,1024]{1,0:T(8,128)}, f32[384,1024]{1,0:T(8,128)})) %all-reduce.15.cloned.1.call-update) | async-done | bytes 3145744 | tf_op jit(solution)/shard_map/psum | solution.py:188
  607.4 40.1 %all-reduce.2 = (f32[1024]{0:T(1024)}, f32[16,512]{1,0:T(8,128)S(1)}, f32[512]{0:T(512)S(1)}, f32[256]{0:T(256)}, f32[1024]{0:T(1024)}) all-reduce(f32[1024]{0:T(1024)S(1)} %fusion.124, f32[16,512]{1,0:T(8,128)S(1)} %convolution_dynamic-update-slice_fusion, ...), channel_id=1, replica_groups=mesh['dp'=2,'context'=4,'tensor'=4] {'dp','context','tensor'}, use_global_device_ids=true, to_apply=%region_31.32 | all-reduce | flops 11008 | bytes 88064 | tf_op jit(solution)/shard_map/psum | solution.py:272
  648.7 1.8 multiply_reduce_fusion
  650.5 3.9 multiply_add_fusion
  654.5 79.4 %all-reduce.13.cloned.1.call-done = f32[1024,16]{0,1:T(8,128)} async-done(((f32[1024,16]{0,1:T(8,128)}), f32[1024,16]{0,1:T(8,128)}) %all-reduce.13.cloned.1.call-update) | async-done | bytes 65552 | tf_op jit(solution)/shard_map/psum | solution.py:272
  733.9 44.3 %reduce-scatter.21.cloned.1.call-done = f32[128,704]{0,1:T(8,128)} async-done(((f32[1024,704]{0,1:T(8,128)}), f32[128,704]{0,1:T(8,128)}) %reduce-scatter.21.cloned.1.call-update) | async-done | bytes 360464 | tf_op jit(solution)/shard_map/reduce_scatter | solution.py:285
  778.2 48.4 %reduce-scatter.23.cloned.1.call-done = f32[128,704]{0,1:T(8,128)} async-done(((f32[1024,704]{0,1:T(8,128)}), f32[128,704]{0,1:T(8,128)}) %reduce-scatter.23.cloned.1.call-update) | async-done | bytes 360464 | tf_op jit(solution)/shard_map/reduce_scatter | solution.py:286
  (455 shorter events, 215.4 us)
Async XLA Ops:
  8.0 4.0 copy-start
  8.0 231.5 %all-reduce.9.cloned.1.call-start = ((), (), s32[]{:S(2)}) async-start(), calls=%async_computation.8 | async-start | bytes 3145728 | tf_op jit(solution)/shard_map/psum | solution.py:183
  9.5 2.9 copy-start.58
  9.5 2.9 copy-start.61
  12.4 27.3 %copy-start.41 = (bf16[128,256]{1,0:T(8,128)(2,1)S(1)}, bf16[128,256]{1,0:T(8,128)(2,1)}, u32[]{:S(2)}) copy-start(bf16[128,256]{1,0:T(8,128)(2,1)} %param.33) | copy-start | bytes 196612
  13.5 94.0 %copy-start.29 = (f32[128,1,3,128]{0,3,2,1:T(8,128)}, f32[128,1,3,128]{0,3,2,1:T(8,128)S(1)}, u32[]{:S(2)}) copy-start(f32[128,1,3,128]{0,3,2,1:T(8,128)S(1)} %copy.99) | copy-start | bytes 589828
  39.0 25.7 %copy-start.49 = (bf16[128,128]{1,0:T(8,128)(2,1)S(1)}, bf16[128,128]{1,0:T(8,128)(2,1)}, u32[]{:S(2)}) copy-start(bf16[128,128]{1,0:T(8,128)(2,1)} %param.32) | copy-start | bytes 98308
  64.3 24.5 %copy-start.15 = (bf16[1024,256]{1,0:T(8,128)(2,1)}, bf16[1024,256]{1,0:T(8,128)(2,1)S(1)}, u32[]{:S(2)}) copy-start(bf16[1024,256]{1,0:T(8,128)(2,1)S(1)} %all_gather.51) | copy-start | bytes 1572868
  96.8 18.7 %copy-start.5 = (f32[6,1,64,256]{3,2,1,0:T(8,128)}, f32[6,1,64,256]{3,2,1,0:T(8,128)S(1)}, u32[]{:S(2)}) copy-start(f32[6,1,64,256]{3,2,1,0:T(8,128)S(1)} %get-tuple-element.1961) | copy-start | bytes 1179652
  96.8 18.7 %copy-start.6 = (f32[6,1,64,128]{3,2,1,0:T(8,128)}, f32[6,1,64,128]{3,2,1,0:T(8,128)S(1)}, u32[]{:S(2)}) copy-start(f32[6,1,64,128]{3,2,1,0:T(8,128)S(1)} %get-tuple-element.1963) | copy-start | bytes 589828
  108.2 8.0 copy-start.31
  108.2 7.9 copy-start.40
  115.9 26.3 %copy-start.50 = (f32[4,1,128]{2,1,0:T(1,128)}, f32[4,1,128]{2,1,0:T(1,128)S(1)}, u32[]{:S(2)}) copy-start(f32[4,1,128]{2,1,0:T(1,128)S(1)} %get-tuple-element.1997) | copy-start | bytes 6148
  116.2 25.9 %copy-start.43 = (bf16[128,256]{1,0:T(8,128)(2,1)S(1)}, bf16[128,256]{1,0:T(8,128)(2,1)}, u32[]{:S(2)}) copy-start(bf16[128,256]{1,0:T(8,128)(2,1)} %param.35) | copy-start | bytes 196612
  116.9 50.0 %copy-start.11 = (f32[384,1,256]{0,2,1:T(8,128)}, f32[384,1,256]{0,2,1:T(8,128)S(1)}, u32[]{:S(2)}) copy-start(f32[384,1,256]{0,2,1:T(8,128)S(1)} %get-tuple-element.1254) | copy-start | bytes 1179652
  116.9 50.0 %copy-start.53 = (f32[384]{0:T(512)}, f32[384]{0:T(512)S(1)}, u32[]{:S(2)}) copy-start(f32[384]{0:T(512)S(1)} %get-tuple-element.1253) | copy-start | bytes 4612
  116.9 49.8 %copy-start.55 = (f32[256]{0:T(256)S(1)}, f32[256]{0:T(256)}, u32[]{:S(2)}) copy-start(f32[256]{0:T(256)} %param.39) | copy-start | bytes 3076
  141.7 25.3 %copy-start.17 = (bf16[1024,256]{1,0:T(8,128)(2,1)}, bf16[1024,256]{1,0:T(8,128)(2,1)S(1)}, u32[]{:S(2)}) copy-start(bf16[1024,256]{1,0:T(8,128)(2,1)S(1)} %all_gather.56) | copy-start | bytes 1572868
  142.2 24.8 %copy-start.13 = (f32[384,256]{0,1:T(8,128)}, f32[384,256]{0,1:T(8,128)S(1)}, u32[]{:S(2)}) copy-start(f32[384,256]{0,1:T(8,128)S(1)} %fusion.169) | copy-start | bytes 1179652
  169.9 69.7 %copy-start.1 = (bf16[384,1024]{1,0:T(8,128)(2,1)S(1)}, bf16[384,1024]{1,0:T(8,128)(2,1)}, u32[]{:S(2)}) copy-start(bf16[384,1024]{1,0:T(8,128)(2,1)} %param.27) | copy-start | bytes 2359300
  169.9 71.5 %copy-start.47 = (f32[1024]{0:T(1024)S(1)}, f32[1024]{0:T(1024)}, u32[]{:S(2)}) copy-start(f32[1024]{0:T(1024)} %param.40) | copy-start | bytes 12292
  169.9 72.7 %all-gather.6.cloned.1.call-start = ((), (), s32[]{:S(2)}) async-start(), calls=%async_computation.9 | async-start | bytes 1622016 | tf_op jit(solution)/shard_map/all_gather | solution.py:151
  170.5 76.3 %all-gather.8.cloned.1.call-start = ((), (), s32[]{:S(2)}) async-start(), calls=%async_computation.10 | async-start | bytes 1622016 | tf_op jit(solution)/shard_map/all_gather | solution.py:152
  171.1 80.5 %all-gather.10.cloned.1.call-start = ((), (), s32[]{:S(2)}) async-start(), calls=%async_computation.11 | async-start | bytes 1622016 | tf_op jit(solution)/shard_map/all_gather | solution.py:153
  171.7 157.3 %all-reduce.11.cloned.1.call-start = ((), (), s32[]{:S(2)}) async-start(), calls=%async_computation.12 | async-start | bytes 3145728 | tf_op jit(solution)/shard_map/psum | solution.py:205
  242.6 86.3 %copy-start.2 = (f32[384,1024]{1,0:T(8,128)}, f32[384,1024]{1,0:T(8,128)S(1)}, u32[]{:S(2)}) copy-start(f32[384,1024]{1,0:T(8,128)S(1)} %get-tuple-element.1225) | copy-start | bytes 4718596
  251.6 4.4 copy-start.60
  259.8 346.4 %all-reduce.15.cloned.1.call-start = ((), (), s32[]{:S(2)}) async-start(), calls=%async_computation.22 | async-start | bytes 6291456 | tf_op jit(solution)/shard_map/psum | solution.py:188
  328.9 2.1 copy-start.22
  328.9 2.1 copy-start.52
  331.0 2.0 copy-start.20
  331.0 2.0 copy-start.56
  476.5 5.1 copy-start.59
  478.4 3.3 copy-start.38
  480.3 2.8 copy-start.26
  480.3 2.9 copy-start.39
  486.7 247.2 %all-reduce.13.cloned.1.call-start = ((), (), s32[]{:S(2)}) async-start(), calls=%async_computation.18 | async-start | bytes 131072 | tf_op jit(solution)/shard_map/psum | solution.py:272
  487.6 246.3 %reduce-scatter.9.cloned.1.call-start = ((), (), s32[]{:S(2)}) async-start(), calls=%async_computation.13 | async-start | bytes 589824 | tf_op jit(solution)/shard_map/reduce_scatter | solution.py:279
  489.8 244.1 %reduce-scatter.11.cloned.1.call-start = ((), (), s32[]{:S(2)}) async-start(), calls=%async_computation.14 | async-start | bytes 589824 | tf_op jit(solution)/shard_map/reduce_scatter | solution.py:280
  492.0 241.9 %reduce-scatter.13.cloned.1.call-start = ((), (), s32[]{:S(2)}) async-start(), calls=%async_computation.15 | async-start | bytes 1179648 | tf_op jit(solution)/shard_map/reduce_scatter | solution.py:281
  494.5 239.4 %reduce-scatter.17.cloned.1.call-start = ((), (), s32[]{:S(2)}) async-start(), calls=%async_computation.17 | async-start | bytes 1179648 | tf_op jit(solution)/shard_map/reduce_scatter | solution.py:283
  497.0 236.9 %reduce-scatter.15.cloned.1.call-start = ((), (), s32[]{:S(2)}) async-start(), calls=%async_computation.16 | async-start | bytes 1179648 | tf_op jit(solution)/shard_map/reduce_scatter | solution.py:282
  498.8 235.2 %reduce-scatter.19.cloned.1.call-start = ((), (), s32[]{:S(2)}) async-start(), calls=%async_computation.19 | async-start | bytes 3244032 | tf_op jit(solution)/shard_map/reduce_scatter | solution.py:284
  503.5 274.8 %reduce-scatter.21.cloned.1.call-start = ((), (), s32[]{:S(2)}) async-start(), calls=%async_computation.20 | async-start | bytes 3244032 | tf_op jit(solution)/shard_map/reduce_scatter | solution.py:285
  507.1 319.5 %reduce-scatter.23.cloned.1.call-start = ((), (), s32[]{:S(2)}) async-start(), calls=%async_computation.21 | async-start | bytes 3244032 | tf_op jit(solution)/shard_map/reduce_scatter | solution.py:286
  511.9 95.5 %copy-start.57 = (f32[256]{0:T(256)S(1)}, f32[256]{0:T(256)}, u32[]{:S(2)}) copy-start(f32[256]{0:T(256)} %get-tuple-element.1105) | copy-start | bytes 3076
  511.9 136.8 %copy-start.46 = (f32[1024]{0:T(1024)S(1)}, f32[1024]{0:T(1024)}, u32[]{:S(2)}) copy-start(f32[1024]{0:T(1024)} %param.30) | copy-start | bytes 12292
  647.5 3.0 copy-start.4
  (29 other events, 35.2 us)
Sparse Core Ops, SparseCore 0:
  170.0 69.4 all-reduce.8
  259.9 68.9 all-reduce.10
  486.8 119.3 all-reduce.14
  612.3 121.5 all-reduce.12
Sparse Core Ops, SparseCore 1:
  172.3 25.6 all-gather.5
  199.7 25.0 all-gather.7
  226.5 25.0 all-gather.9
  492.0 32.4 reduce-scatter.8
  528.2 34.1 reduce-scatter.10
  566.1 35.9 reduce-scatter.12
  605.7 35.9 reduce-scatter.16
  645.2 35.9 reduce-scatter.14
  685.1 44.6 reduce-scatter.18
  733.7 44.5 reduce-scatter.20
  782.1 44.5 reduce-scatter.22
where the time goes:
time: 843 us; the launch traced here: 835 us
  waiting for transfers between devices  343 us (41%)
  blocking collectives  192 us (23%)
  matrix products  140 us (17%)
  other arithmetic  77.7 us (9%)
  local copies, waits for them, and re-layouts  64.1 us (8%)
  between operations  16.4 us (2%)
    psum x1, waiting for transfers between devices, local(): result = hidden + lax.psum(project_back(product, fetched[7]), 'tensor')  92.7 us
    psum x1, waiting for transfers between devices, local(): lax.psum((gain_one_part, gain_two_part, grad_head, grad_lowrank, rank_ful...  79.4 us
    psum x1, waiting for transfers between devices, local(): hidden = stream + lax.psum(project_back(gated, fetched[4]), 'tensor')  67.8 us
    reduce_scatter x1, waiting for transfers between devices, local(): lax.psum_scatter(grad_down, ('dp', 'context'), scatter_dimension=0, tiled...  48.4 us
    reduce_scatter x1, waiting for transfers between devices, local(): lax.psum_scatter(grad_up, ('dp', 'context'), scatter_dimension=0, tiled=T...  44.3 us
    psum x1, blocking collectives, local(): lax.psum((gain_one_part, gain_two_part, grad_head, grad_lowrank, rank_ful...  40.1 us
    dot_general x24, matrix products, advance(): scores = jnp.dot(query_up, key_down.T, precision=highest_precision) * causal  29.7 us
    all_gather x3, blocking collectives, carried_in(): pieces = jax.tree.map(lambda part: lax.all_gather(part, axis), value)  28.6 us
  transfers between devices with their start and end apart: 15, of which 7 were waited for; matrix products, arithmetic and copies ran while one was open for 12% of the time, Pallas kernels for 0%

commit v1 on v0

--- a/solution.py
+++ b/solution.py
@@ -270,8 +270,10 @@
     )
     bias_full = lax.dynamic_update_slice(jnp.zeros((DK,), jnp.float32), grad_bias, (offset,))
     summed = lax.psum(
-        (gain_one_part, gain_two_part, grad_head, grad_lowrank, rank_full, bias_full),
-        ("dp", "context", "tensor"),
+        lax.psum(
+            (gain_one_part, gain_two_part, grad_head, grad_lowrank, rank_full, bias_full), "dp"
+        ),
+        ("context", "tensor"),
     )
     rankup_shard = lax.dynamic_slice(summed[4], (0, offset), (RANK, columns))
     bias_shard = lax.dynamic_slice(summed[5], (offset,), (columns,))

time: 843 us -> 864 us (1.025)
  blocking collectives: 192 us -> 231 us
  waiting for transfers between devices: 343 us -> 318 us
    psum x0 -> x1, blocking collectives: none -> 76.1 us  [local(): lax.psum(lax.psum((gain_one_part, gain_two_part, grad_head, grad_lowrank,...]
    psum x1, waiting for transfers between devices: 79.4 us -> 11.6 us  [local(): lax.psum((gain_one_part, gain_two_part, grad_head, grad_lowrank, rank_ful...]
    psum x1, blocking collectives: 40.1 us -> 3.53 us  [local(): lax.psum((gain_one_part, gain_two_part, grad_head, grad_lowrank, rank_ful...]
    psum x0 -> x1, waiting for transfers between devices: none -> 23.5 us  [local(): lax.psum(lax.psum((gain_one_part, gain_two_part, grad_head, grad_lowrank,...]
    reduce_scatter x1, waiting for transfers between devices: 0.02 us -> 8.8 us  [local(): lax.psum_scatter(grad_gate, ('dp', 'context'), scatter_dimension=0, tiled...]
  transfers between devices with their start and end apart: 15 -> 16, of which waited for: 7 -> 9; matrix products, arithmetic and copies ran while one was open for 12% -> 13% of each run, Pallas kernels for 0% -> 0%
where the time goes in v1:
time: 864 us; the launch traced here: 857 us
  waiting for transfers between devices  318 us (37%)
  blocking collectives  231 us (27%)
  matrix products  148 us (17%)
  other arithmetic  78.1 us (9%)
  local copies, waits for them, and re-layouts  63.5 us (7%)
  between operations  16.4 us (2%)
    psum x1, waiting for transfers between devices, local(): result = hidden + lax.psum(project_back(product, fetched[7]), 'tensor')  98.8 us
    psum x1, blocking collectives, local(): lax.psum(lax.psum((gain_one_part, gain_two_part, grad_head, grad_lowrank,...  76.1 us
    psum x1, waiting for transfers between devices, local(): hidden = stream + lax.psum(project_back(gated, fetched[4]), 'tensor')  67.7 us
    reduce_scatter x1, waiting for transfers between devices, local(): lax.psum_scatter(grad_up, ('dp', 'context'), scatter_dimension=0, tiled=T...  48.6 us
    reduce_scatter x1, waiting for transfers between devices, local(): lax.psum_scatter(grad_down, ('dp', 'context'), scatter_dimension=0, tiled...  48.4 us
    dot_general x24, matrix products, advance(): scores = jnp.dot(query_up, key_down.T, precision=highest_precision) * causal  29.7 us
    all_gather x3, blocking collectives, carried_in(): pieces = jax.tree.map(lambda part: lax.all_gather(part, axis), value)  28.7 us
    all_gather x1, blocking collectives, local(): lax.all_gather(query_weight, ('dp', 'context'), axis=0, tiled=True)  25.4 us
  transfers between devices with their start and end apart: 16, of which 9 were waited for; matrix products, arithmetic and copies ran while one was open for 13% of the time, Pallas kernels for 0%

profile of v1, /device:TPU:0, one launch (start us, length us, event | category | flops | bytes accessed | tf_op | source)
XLA Modules:
  0.0 856.9 jit_solution(4906647837908122816)
XLA Ops:
  9.5 2.5 convert_multiply_fusion
  13.6 25.4 %all_gather.52 = bf16[1024,128]{1,0:T(8,128)(2,1)S(1)} all-gather(bf16[128,128]{1,0:T(8,128)(2,1)S(1)} %copy-done.48), channel_id=1, replica_groups=mesh['dp'=2,'context'=4,'tensor'=4] {'dp','context'}, dimensions={0}, use_global_device_ids=true | all-gather | bytes 294912 | tf_op jit(solution)/shard_map/all_gather | solution.py:146
  39.7 24.6 %all_gather.51 = bf16[1024,256]{1,0:T(8,128)(2,1)S(1)} all-gather(bf16[128,256]{1,0:T(8,128)(2,1)S(1)} %copy-done.41), channel_id=1, replica_groups=mesh['dp'=2,'context'=4,'tensor'=4] {'dp','context'}, dimensions={0}, use_global_device_ids=true | all-gather | bytes 589824 | tf_op jit(solution)/shard_map/all_gather | solution.py:148
  64.7 23.7 %all_gather.50 = bf16[1024,128]{1,0:T(8,128)(2,1)S(1)} all-gather(bf16[128,128]{1,0:T(8,128)(2,1)S(1)} %copy-done.49), channel_id=1, replica_groups=mesh['dp'=2,'context'=4,'tensor'=4] {'dp','context'}, dimensions={0}, use_global_device_ids=true | all-gather | bytes 294912 | tf_op jit(solution)/shard_map/all_gather | solution.py:147
  89.1 7.0 while.106
  96.8 10.7 %all-gather = f32[4,128,256]{2,1,0:T(8,128)S(1)} all-gather(f32[1,128,256]{2,1,0:T(8,128)S(1)} %get-tuple-element.770), channel_id=2, replica_groups=mesh['dp'=2,'context'=4,'tensor'=4] {'context'}, dimensions={0}, use_global_device_ids=true | all-gather | bytes 655360 | tf_op jit(solution)/shard_map/all_gather | solution.py:17
  108.3 7.2 all_gather.53
  117.0 24.7 %all_gather.56 = bf16[1024,256]{1,0:T(8,128)(2,1)S(1)} all-gather(bf16[128,256]{1,0:T(8,128)(2,1)S(1)} %copy-done.42), channel_id=1, replica_groups=mesh['dp'=2,'context'=4,'tensor'=4] {'dp','context'}, dimensions={0}, use_global_device_ids=true | all-gather | bytes 589824 | tf_op jit(solution)/shard_map/all_gather | solution.py:149
  142.2 24.5 %all_gather.57 = bf16[1024,256]{1,0:T(8,128)(2,1)S(1)} all-gather(bf16[128,256]{1,0:T(8,128)(2,1)S(1)} %copy-done.43), channel_id=1, replica_groups=mesh['dp'=2,'context'=4,'tensor'=4] {'dp','context'}, dimensions={0}, use_global_device_ids=true | all-gather | bytes 589824 | tf_op jit(solution)/shard_map/all_gather | solution.py:150
  171.8 67.7 %all-reduce.11.cloned.1.call-done = f32[384,1024]{1,0:T(8,128)} async-done(((f32[384,1024]{1,0:T(8,128)}), f32[384,1024]{1,0:T(8,128)}) %all-reduce.11.cloned.1.call-update) | async-done | bytes 1572880 | tf_op jit(solution)/shard_map/psum | solution.py:183
  239.5 1.8 multiply_reduce_fusion.2
  242.6 4.2 fusion.171
  246.8 3.5 fusion.172
  251.6 4.4 multiply_convert_fusion.2
  257.7 2.0 convolution_add_fusion.3
  262.8 53.1 %while.109 = (s32[]{:T(128)}, f32[1,128,256]{2,1,0:T(8,128)S(1)}, f32[6,1,64,128]{3,2,1,0:T(8,128)}, f32[6,1,64,128]{3,2,1,0:T(8,128)}, f32[6,1,128,64]{2,3,1,0:...) while((s32[]{:T(128)}, f32[1,128,256]{2,1,0:T(8,128)S(1)}, ...), condition=%wide.region_19.20_spmd.clone.clone, body=%wide.region_17.19_spmd.clone.sunk.clone | while | flops 32215044 | bytes 1288872 | solution.py:90
  317.9 3.5 fusion.173
  321.4 7.5 all-reduce.13.cloned.1.call-done
  328.9 1.8 multiply_reduce_fusion.1
  331.0 1.9 multiply_add_fusion.1
  336.5 10.7 %all-gather.1 = f32[512,256]{1,0:T(8,128)} all-gather(f32[128,256]{1,0:T(8,128)S(1)} %fusion.128), channel_id=3, replica_groups=mesh['dp'=2,'context'=4,'tensor'=4] {'context'}, dimensions={0}, use_global_device_ids=true | all-gather | bytes 655360 | tf_op jit(solution)/shard_map/all_gather | solution.py:17
  347.2 1.9 rev.7
  349.1 3.1 while.108
  354.8 1.9 copy.112
  356.8 2.5 fusion.125
  361.3 115.2 %while.105 = (s32[]{:T(128)}, f32[1,128,256]{1,2,0:T(8,128)S(1)}, f32[6,1,64,128]{3,2,1,0:T(8,128)}, bf16[6,1,64,128]{3,2,1,0:T(8,128)(2,1)}, bf16[6,1,64,256]{3...) while((s32[]{:T(128)}, f32[1,128,256]{1,2,0:T(8,128)S(1)}, ...), condition=%wide.region_24.25_spmd.clone.clone, body=%wide.region_20.24_spmd.clone.sunk.clone | while | flops 139243520 | bytes 3109597 | solution.py:90
  378.8 1.7 fusion.345
  436.4 1.7 fusion.345
  476.5 1.9 fusion.144
  481.8 2.6 fusion.175
  490.0 4.4 add_add_fusion
  494.5 11.6 %all-reduce.15.cloned.1.call-done = f32[1024,16]{0,1:T(8,128)} async-done(((f32[1024,16]{0,1:T(8,128)}), f32[1024,16]{0,1:T(8,128)}) %all-reduce.15.cloned.1.call-update) | async-done | bytes 65552 | tf_op jit(solution)/shard_map/psum | solution.py:273
  506.2 2.1 fusion.178
  508.4 2.1 fusion.179
  510.5 2.4 fusion.180
  513.0 2.4 fusion.132
  518.3 3.5 fusion.182
  521.9 3.6 fusion.183
  526.7 3.6 convolution_bitcast_fusion.5
  531.9 98.8 %all-reduce.19.cloned.1.call-done = (f32[384,1024]{1,0:T(8,128)}, f32[384,1024]{1,0:T(8,128)}) async-done(((f32[384,1024]{1,0:T(8,128)}, f32[384,1024]{1,0:T(8,128)}), (f32[384,1024]{1,0:T(8,128)}, f32[384,1024]{1,0:T(8,128)})) %all-reduce.19.cloned.1.call-update) | async-done | bytes 3145744 | tf_op jit(solution)/shard_map/psum | solution.py:188
  631.9 3.5 all-reduce.4
  635.4 76.1 %all-reduce.2 = (f32[1024]{0:T(1024)}, f32[16,512]{1,0:T(8,128)S(1)}, f32[512]{0:T(512)S(1)}, f32[256]{0:T(256)}, f32[1024]{0:T(1024)}) all-reduce(f32[1024]{0:T(1024)S(1)} %get-tuple-element.1222, f32[16,512]{1,0:T(8,128)S(1)} %get-tuple-element.1223, ...), channel_id=1, replica_groups=mesh['dp'=2,'context'=4,'tensor'=4] {'context','tensor'}, use_global_device_ids=true, to_apply=%region_32.33 | all-reduce | flops 11008 | bytes 88064 | tf_op jit(solution)/shard_map/psum | solution.py:272
  712.7 1.9 multiply_reduce_fusion
  714.7 4.1 multiply_add_fusion
  718.8 23.5 %all-reduce.17.cloned.1.call-done = f32[1024,16]{0,1:T(8,128)} async-done(((f32[1024,16]{0,1:T(8,128)}), f32[1024,16]{0,1:T(8,128)}) %all-reduce.17.cloned.1.call-update) | async-done | bytes 65552 | tf_op jit(solution)/shard_map/psum | solution.py:272
  742.3 8.8 %reduce-scatter.19.cloned.1.call-done = f32[128,704]{0,1:T(8,128)} async-done(((f32[1024,704]{0,1:T(8,128)}), f32[128,704]{0,1:T(8,128)}) %reduce-scatter.19.cloned.1.call-update) | async-done | bytes 360464 | tf_op jit(solution)/shard_map/reduce_scatter | solution.py:286
  751.1 48.6 %reduce-scatter.21.cloned.1.call-done = f32[128,704]{0,1:T(8,128)} async-done(((f32[1024,704]{0,1:T(8,128)}), f32[128,704]{0,1:T(8,128)}) %reduce-scatter.21.cloned.1.call-update) | async-done | bytes 360464 | tf_op jit(solution)/shard_map/reduce_scatter | solution.py:287
  799.7 48.4 %reduce-scatter.23.cloned.1.call-done = f32[128,704]{0,1:T(8,128)} async-done(((f32[1024,704]{0,1:T(8,128)}), f32[128,704]{0,1:T(8,128)}) %reduce-scatter.23.cloned.1.call-update) | async-done | bytes 360464 | tf_op jit(solution)/shard_map/reduce_scatter | solution.py:288
  (459 shorter events, 223.9 us)
Async XLA Ops:
  8.0 4.0 copy-start
  8.0 231.5 %all-reduce.11.cloned.1.call-start = ((), (), s32[]{:S(2)}) async-start(), calls=%async_computation.8 | async-start | bytes 3145728 | tf_op jit(solution)/shard_map/psum | solution.py:183
  9.5 2.9 copy-start.58
  9.5 2.9 copy-start.61
  12.4 27.3 %copy-start.41 = (bf16[128,256]{1,0:T(8,128)(2,1)S(1)}, bf16[128,256]{1,0:T(8,128)(2,1)}, u32[]{:S(2)}) copy-start(bf16[128,256]{1,0:T(8,128)(2,1)} %param.33) | copy-start | bytes 196612
  13.5 94.1 %copy-start.29 = (f32[128,1,3,128]{0,3,2,1:T(8,128)}, f32[128,1,3,128]{0,3,2,1:T(8,128)S(1)}, u32[]{:S(2)}) copy-start(f32[128,1,3,128]{0,3,2,1:T(8,128)S(1)} %copy.99) | copy-start | bytes 589828
  39.0 25.7 %copy-start.49 = (bf16[128,128]{1,0:T(8,128)(2,1)S(1)}, bf16[128,128]{1,0:T(8,128)(2,1)}, u32[]{:S(2)}) copy-start(bf16[128,128]{1,0:T(8,128)(2,1)} %param.32) | copy-start | bytes 98308
  64.3 24.5 %copy-start.15 = (bf16[1024,256]{1,0:T(8,128)(2,1)}, bf16[1024,256]{1,0:T(8,128)(2,1)S(1)}, u32[]{:S(2)}) copy-start(bf16[1024,256]{1,0:T(8,128)(2,1)S(1)} %all_gather.51) | copy-start | bytes 1572868
  96.8 18.7 %copy-start.5 = (f32[6,1,64,256]{3,2,1,0:T(8,128)}, f32[6,1,64,256]{3,2,1,0:T(8,128)S(1)}, u32[]{:S(2)}) copy-start(f32[6,1,64,256]{3,2,1,0:T(8,128)S(1)} %get-tuple-element.1967) | copy-start | bytes 1179652
  96.8 18.7 %copy-start.6 = (f32[6,1,64,128]{3,2,1,0:T(8,128)}, f32[6,1,64,128]{3,2,1,0:T(8,128)S(1)}, u32[]{:S(2)}) copy-start(f32[6,1,64,128]{3,2,1,0:T(8,128)S(1)} %get-tuple-element.1969) | copy-start | bytes 589828
  108.3 8.0 copy-start.31
  108.3 7.9 copy-start.40
  116.0 26.3 %copy-start.50 = (f32[4,1,128]{2,1,0:T(1,128)}, f32[4,1,128]{2,1,0:T(1,128)S(1)}, u32[]{:S(2)}) copy-start(f32[4,1,128]{2,1,0:T(1,128)S(1)} %get-tuple-element.2006) | copy-start | bytes 6148
  116.3 25.9 %copy-start.43 = (bf16[128,256]{1,0:T(8,128)(2,1)S(1)}, bf16[128,256]{1,0:T(8,128)(2,1)}, u32[]{:S(2)}) copy-start(bf16[128,256]{1,0:T(8,128)(2,1)} %param.35) | copy-start | bytes 196612
  117.0 50.0 %copy-start.11 = (f32[384,1,256]{0,2,1:T(8,128)}, f32[384,1,256]{0,2,1:T(8,128)S(1)}, u32[]{:S(2)}) copy-start(f32[384,1,256]{0,2,1:T(8,128)S(1)} %get-tuple-element.1259) | copy-start | bytes 1179652
  117.0 50.0 %copy-start.53 = (f32[384]{0:T(512)}, f32[384]{0:T(512)S(1)}, u32[]{:S(2)}) copy-start(f32[384]{0:T(512)S(1)} %get-tuple-element.1258) | copy-start | bytes 4612
  117.0 49.8 %copy-start.55 = (f32[256]{0:T(256)S(1)}, f32[256]{0:T(256)}, u32[]{:S(2)}) copy-start(f32[256]{0:T(256)} %param.39) | copy-start | bytes 3076
  141.7 25.2 %copy-start.17 = (bf16[1024,256]{1,0:T(8,128)(2,1)}, bf16[1024,256]{1,0:T(8,128)(2,1)S(1)}, u32[]{:S(2)}) copy-start(bf16[1024,256]{1,0:T(8,128)(2,1)S(1)} %all_gather.56) | copy-start | bytes 1572868
  142.2 24.7 %copy-start.13 = (f32[384,256]{0,1:T(8,128)}, f32[384,256]{0,1:T(8,128)S(1)}, u32[]{:S(2)}) copy-start(f32[384,256]{0,1:T(8,128)S(1)} %fusion.169) | copy-start | bytes 1179652
  169.9 69.7 %copy-start.1 = (bf16[384,1024]{1,0:T(8,128)(2,1)S(1)}, bf16[384,1024]{1,0:T(8,128)(2,1)}, u32[]{:S(2)}) copy-start(bf16[384,1024]{1,0:T(8,128)(2,1)} %param.27) | copy-start | bytes 2359300
  169.9 71.5 %copy-start.47 = (f32[1024]{0:T(1024)S(1)}, f32[1024]{0:T(1024)}, u32[]{:S(2)}) copy-start(f32[1024]{0:T(1024)} %param.40) | copy-start | bytes 12292
  169.9 72.7 %all-gather.6.cloned.1.call-start = ((), (), s32[]{:S(2)}) async-start(), calls=%async_computation.9 | async-start | bytes 1622016 | tf_op jit(solution)/shard_map/all_gather | solution.py:151
  170.5 76.3 %all-gather.8.cloned.1.call-start = ((), (), s32[]{:S(2)}) async-start(), calls=%async_computation.10 | async-start | bytes 1622016 | tf_op jit(solution)/shard_map/all_gather | solution.py:152
  171.1 80.5 %all-gather.10.cloned.1.call-start = ((), (), s32[]{:S(2)}) async-start(), calls=%async_computation.11 | async-start | bytes 1622016 | tf_op jit(solution)/shard_map/all_gather | solution.py:153
  171.7 157.2 %all-reduce.13.cloned.1.call-start = ((), (), s32[]{:S(2)}) async-start(), calls=%async_computation.12 | async-start | bytes 3145728 | tf_op jit(solution)/shard_map/psum | solution.py:205
  242.6 86.3 %copy-start.2 = (f32[384,1024]{1,0:T(8,128)}, f32[384,1024]{1,0:T(8,128)S(1)}, u32[]{:S(2)}) copy-start(f32[384,1024]{1,0:T(8,128)S(1)} %get-tuple-element.1230) | copy-start | bytes 4718596
  251.6 4.4 copy-start.60
  259.8 246.3 %all-reduce.15.cloned.1.call-start = ((), (), s32[]{:S(2)}) async-start(), calls=%async_computation.18 | async-start | bytes 131072 | tf_op jit(solution)/shard_map/psum | solution.py:273
  328.9 2.1 copy-start.52
  476.5 5.1 copy-start.59
  478.5 3.3 copy-start.38
  480.3 4.0 copy-start.26
  480.3 4.0 copy-start.39
  481.8 4.1 copy-start.16
  481.8 4.1 copy-start.35
  489.9 140.8 %all-reduce.19.cloned.1.call-start = ((), (), s32[]{:S(2)}) async-start(), calls=%async_computation.23 | async-start | bytes 6291456 | tf_op jit(solution)/shard_map/psum | solution.py:188
  494.4 247.8 %all-reduce.17.cloned.1.call-start = ((), (), s32[]{:S(2)}) async-start(), calls=%async_computation.19 | async-start | bytes 131072 | tf_op jit(solution)/shard_map/psum | solution.py:272
  506.1 236.1 %reduce-scatter.9.cloned.1.call-start = ((), (), s32[]{:S(2)}) async-start(), calls=%async_computation.13 | async-start | bytes 589824 | tf_op jit(solution)/shard_map/reduce_scatter | solution.py:281
  508.3 233.9 %reduce-scatter.11.cloned.1.call-start = ((), (), s32[]{:S(2)}) async-start(), calls=%async_computation.14 | async-start | bytes 589824 | tf_op jit(solution)/shard_map/reduce_scatter | solution.py:282
  510.5 231.8 %reduce-scatter.13.cloned.1.call-start = ((), (), s32[]{:S(2)}) async-start(), calls=%async_computation.15 | async-start | bytes 1179648 | tf_op jit(solution)/shard_map/reduce_scatter | solution.py:283
  513.0 229.3 %reduce-scatter.17.cloned.1.call-start = ((), (), s32[]{:S(2)}) async-start(), calls=%async_computation.17 | async-start | bytes 1179648 | tf_op jit(solution)/shard_map/reduce_scatter | solution.py:285
  515.4 226.8 %reduce-scatter.15.cloned.1.call-start = ((), (), s32[]{:S(2)}) async-start(), calls=%async_computation.16 | async-start | bytes 1179648 | tf_op jit(solution)/shard_map/reduce_scatter | solution.py:284
  517.2 233.9 %reduce-scatter.19.cloned.1.call-start = ((), (), s32[]{:S(2)}) async-start(), calls=%async_computation.20 | async-start | bytes 3244032 | tf_op jit(solution)/shard_map/reduce_scatter | solution.py:286
  521.9 277.8 %reduce-scatter.21.cloned.1.call-start = ((), (), s32[]{:S(2)}) async-start(), calls=%async_computation.21 | async-start | bytes 3244032 | tf_op jit(solution)/shard_map/reduce_scatter | solution.py:287
  525.5 322.5 %reduce-scatter.23.cloned.1.call-start = ((), (), s32[]{:S(2)}) async-start(), calls=%async_computation.22 | async-start | bytes 3244032 | tf_op jit(solution)/shard_map/reduce_scatter | solution.py:288
  530.3 101.6 %copy-start.57 = (f32[256]{0:T(256)S(1)}, f32[256]{0:T(256)}, u32[]{:S(2)}) copy-start(f32[256]{0:T(256)} %get-tuple-element.1105) | copy-start | bytes 3076
  530.3 182.4 %copy-start.46 = (f32[1024]{0:T(1024)S(1)}, f32[1024]{0:T(1024)}, u32[]{:S(2)}) copy-start(f32[1024]{0:T(1024)} %param.30) | copy-start | bytes 12292
  711.5 3.1 copy-start.4
  (30 other events, 38.5 us)
Sparse Core Ops, SparseCore 0:
  170.0 69.4 all-reduce.10
  259.9 68.9 all-reduce.12
  490.0 16.0 all-reduce.14
  508.4 122.2 all-reduce.18
  636.0 106.1 all-reduce.16
Sparse Core Ops, SparseCore 1:
  172.3 25.5 all-gather.5
  199.6 25.0 all-gather.7
  226.5 25.0 all-gather.9
  510.6 35.3 reduce-scatter.8
  549.6 34.0 reduce-scatter.10
  587.5 35.9 reduce-scatter.12
  627.0 35.9 reduce-scatter.16
  666.7 35.9 reduce-scatter.14
  706.5 44.5 reduce-scatter.18
  755.1 44.5 reduce-scatter.20
  803.5 44.5 reduce-scatter.22
